TPU v7x, 256 devices: a whole 4x4x8 slice. The times are simulated.
256 devices in a mesh: col: 16 (over z, core), tile: 16 (over y, x).
Axes of the slice: x: 4, y: 4, z: 8, core: 2. Of those that a mesh axis runs over, the one named last changes fastest.
Arguments:
- boundary: bfloat16 [16, 1024, 4, 1024], P('col', 'tile'), may hold values from -6 to 6
- row_tensors: bfloat16 [16, 4, 4, 4, 4], P('col'), may hold values from -3 to 3
- sketch_bond: bfloat16 [16, 1024, 1024], P('col', 'tile'), may hold values from -0.1875 to 0.1875
- sketch_phys: bfloat16 [16, 4, 4, 1024], P('col'), may hold values from -6 to 6
- edge_factor: bfloat16 [1024, 4, 1024], P('tile'), may hold values from -0.09375 to 0.09375
- closing: float32 [16, 4], P('col'), may hold values from 0.2 to 2
- left_edge: float32 [1024], replicated, may hold values from -6 to 6
Outputs:
- new_boundary: bfloat16 [16, 1024, 4, 1024], P('col', 'tile')
- envs: float32 [16, 1024], P('col', 'tile')
All inputs are finite; a program needn't handle non-finite values.
Results may differ from a plain program's by a relative error of at most 0.012.
The roundings to bfloat16 on the way count: a program that leaves them out, or rounds other values in their place, can miss the bound.
Values may be sent and summed in bfloat16 or wider, within the bound.
A program may use at most 128 MiB of HBM per device.

v0:
```python
import functools

import jax
import jax.numpy as jnp
from jax import lax
from jax.experimental import pallas as pl
from jax.experimental.pallas import tpu as pltpu
from jax.sharding import PartitionSpec as P

GRAM_SHIFT = 0.001
NB = 128
OWNER = 0
SIDE = 4
HIGHEST = lax.Precision.HIGHEST
MESH = pl.DeviceIdType.MESH
VMEM = pl.BlockSpec(memory_space=pltpu.VMEM)


def f32_dot(x, y, dims=(((1,), (0,)), ((), ()))):
    return lax.dot_general(x, y, dims, precision=HIGHEST, preferred_element_type=jnp.float32)


def factor_block(block, inv_ref):
    sub = lax.broadcasted_iota(jnp.int32, (8, NB), 0)
    lane = lax.broadcasted_iota(jnp.int32, (8, NB), 1)
    a0 = tuple(block[8 * i:8 * i + 8, :] for i in range(16))
    m0 = tuple((lane == sub + 8 * i).astype(jnp.float32) for i in range(16))

    def along(x, t):
        return jnp.broadcast_to(x[:, t:t + 1], (8, NB))

    def down(x, t):
        return jnp.broadcast_to(x[t:t + 1, :], (8, NB))

    def tree(terms):
        while len(terms) > 1:
            terms = [terms[i] + terms[i + 1] for i in range(0, len(terms), 2)]
        return terms[0]

    def group(count, g, carry):
        a, m, c = list(carry[0]), list(carry[1]), list(carry[2])
        p, n = a[0], m[0]
        done = jnp.zeros((8, NB), jnp.float32)
        for s in range(8):
            here = sub == s
            pivot = down(c[s], s)
            inv = 1.0 / pivot
            nrow = down(n, s)
            done = jnp.where(here, nrow * lax.rsqrt(pivot), done)
            column = c[s]

            def step(x, row):
                row = row * inv
                return jnp.where(here, row, x - column * row)

            for t in range(s + 1, 8):
                c[t] = step(c[t], down(c[t], s))
            p = step(p, down(p, s))
            n = step(n, nrow)
        inv_ref[pl.ds(pl.multiple_of(g * 8, 8), 8), :] = done
        prow = [down(p, t) for t in range(8)]
        nrow = [down(n, t) for t in range(8)]
        for i in range(1, count):
            x = [along(a[i], t) for t in range(8)]
            a[i] = a[i] - tree([x[t] * prow[t] for t in range(8)])
            m[i] = m[i] - tree([x[t] * nrow[t] for t in range(8)])
            if i == 1:
                c = [along(a[1], 8 + t) for t in range(8)]
        zero = jnp.zeros((8, NB), jnp.float32)
        return tuple(pltpu.roll(x, NB - 8, 1) for x in a[1:]) + (zero,), tuple(m[1:]) + (zero,), tuple(c)

    carry = (a0, m0, tuple(along(a0[0], t) for t in range(8)))
    for lo in range(0, 16, 4):
        carry = (carry[0][:16 - lo], carry[1][:16 - lo], carry[2])
        carry = lax.fori_loop(lo, lo + 4, functools.partial(group, 16 - lo), carry)


class Place:
    def __init__(self):
        tile = lax.axis_index("tile")
        self.tile = tile
        self.y, self.x = tile // SIDE, tile % SIDE

    def coordinate(self, axis):
        return self.x if axis == 0 else self.y

    def along(self, axis, index):
        return self.y * SIDE + index if axis == 0 else index * SIDE + self.x


def remote(src, dst, send, recv, where):
    return pltpu.make_async_remote_copy(
        src_ref=src, dst_ref=dst, send_sem=send, recv_sem=recv, device_id=where, device_id_type=MESH)


class LineGather:
    def __init__(self, place, axis, own, slot, sems, row=None):
        self.place, self.axis, self.own, self.slot, self.row = place, axis, own, slot, row
        self.send1, self.recv1, self.send2, self.recv2 = sems

    def first(self, s):
        place = self.place
        target = place.along(self.axis, (place.coordinate(self.axis) + s) % SIDE)
        return remote(self.own, self.slot(place.tile), self.send1.at[s - 1], self.recv1.at[s - 1], {"tile": target})

    def second(self, s, j):
        place = self.place
        other = 1 - self.axis
        target = place.along(other, (place.coordinate(other) + s) % SIDE)
        source = place.along(self.axis, (place.coordinate(self.axis) + SIDE - j) % SIDE)
        piece = self.own if j == 0 else self.slot(source)
        return remote(piece, self.slot(source), self.send2.at[s - 1, j], self.recv2.at[s - 1, j], {"tile": target})

    def start(self):
        for s in range(1, SIDE):
            self.first(s).start()

    def forward(self):
        for s in range(1, SIDE):
            self.second(s, 0).start()
        for j in range(1, SIDE):
            self.first(j).wait_recv()
            for s in range(1, SIDE):
                self.second(s, j).start()

    def finish(self):
        for s in range(1, SIDE):
            for j in range(SIDE):
                self.second(s, j).wait_recv()
        for s in range(1, SIDE):
            self.first(s).wait_send()
            for j in range(SIDE):
                self.second(s, j).wait_send()


LINE_SEMS = [
    pltpu.SemaphoreType.DMA((2, SIDE - 1)),
    pltpu.SemaphoreType.DMA((2, SIDE - 1)),
    pltpu.SemaphoreType.DMA((2, SIDE - 1, SIDE)),
    pltpu.SemaphoreType.DMA((2, SIDE - 1, SIDE)),
]


def front_kernel(b_ref, g_ref, phys_ref, q_ref, ball_ref, gall, r_ref, part, total, s_ref, inv_ref, *scratch):
    land, middle, land2, own = scratch[:2], scratch[2:4], scratch[4:6], scratch[6:8]
    sems = scratch[8:]
    g_sems, b_sems = sems[0:4], sems[4:8]
    rs1_send, rs1_recv, rs2_send, rs2_recv, ag1_send, ag1_recv, ag2_send, ag2_recv, here_sem = sems[8:]
    place = Place()
    legs, share, width = b_ref.shape
    barrier = pltpu.get_barrier_semaphore()
    for axis in (0, 1):
        for s in range(1, SIDE):
            target = place.along(axis, (place.coordinate(axis) + s) % SIDE)
            pl.semaphore_signal(barrier, inc=1, device_id={"tile": target}, device_id_type=MESH)
    pl.semaphore_wait(barrier, 2 * (SIDE - 1))

    half = share // 2
    sketch = [
        LineGather(
            place, h, g_ref.at[h * half:h * half + half],
            lambda tile, h=h: gall.at[pl.ds(pl.multiple_of(tile * share + h * half, half), half)],
            [x.at[h] for x in g_sems])
        for h in (0, 1)
    ]
    for gather in sketch:
        gather.start()
    mine = pl.multiple_of(place.tile * share, share)
    gall[pl.ds(mine, share), :] = g_ref[...]
    keep = pltpu.make_async_copy(b_ref, ball_ref.at[:, pl.ds(mine, share), :], here_sem)
    keep.start()
    for gather in sketch:
        gather.forward()
    for gather in sketch:
        gather.finish()

    two = legs // 2
    sites = [
        LineGather(
            place, h, b_ref.at[h * two:h * two + two],
            lambda tile, h=h: ball_ref.at[h * two:h * two + two, pl.ds(pl.multiple_of(tile * share, share), share), :],
            [x.at[h] for x in b_sems])
        for h in (0, 1)
    ]
    keep.wait()
    for gather in sites:
        gather.start()

    for u in range(legs):
        sketched = lax.dot_general(
            b_ref[u], gall[...], (((1,), (1,)), ((), ())), preferred_element_type=jnp.float32)
        for r in range(legs):
            term = sketched * phys_ref[u * legs + r:u * legs + r + 1, :]
            rows = slice(r * share, r * share + share)
            r_ref[rows, :] = term if u == 0 else r_ref[rows, :] + term

    blocks = width // NB
    pairs = blocks // 2
    packed = NB * (blocks + 1)
    cut = NB * (pairs + 1)
    columns = ((0, cut), (cut, packed))

    def view(ref, i):
        lo = 0 if i < pairs else (i + 1) * NB
        return ref.at[i if i < pairs else blocks - 1 - i, :, lo:lo + (blocks - i) * NB]

    flipped = r_ref[...].T
    for i in range(blocks):
        view(part, i)[...] = f32_dot(flipped[i * NB:i * NB + NB, :], r_ref[:, i * NB:])

    strip = NB // SIDE

    def line(h):
        axis = h
        c1, c2 = place.coordinate(axis), place.coordinate(1 - axis)
        lo, hi = columns[h]
        return axis, c1, c2, slice(lo, hi)

    def rs1(h, s):
        axis, c1, c2, cols = line(h)
        p = (c1 + s) % SIDE
        return remote(part.at[p, :, cols], land[h].at[s - 1], rs1_send.at[h, s - 1], rs1_recv.at[h, s - 1],
                      {"tile": place.along(axis, p)})

    def rs2(h, s):
        axis, c1, c2, cols = line(h)
        p = (c2 + s) % SIDE
        return remote(middle[h].at[pl.ds(pl.multiple_of(p * strip, strip), strip)], land2[h].at[s - 1],
                      rs2_send.at[h, s - 1], rs2_recv.at[h, s - 1], {"tile": place.along(1 - axis, p)})

    def ag1(h, s):
        axis, c1, c2, cols = line(h)
        p = (c2 + s) % SIDE
        return remote(own[h], total.at[c1, pl.ds(pl.multiple_of(c2 * strip, strip), strip), cols],
                      ag1_send.at[h, s - 1], ag1_recv.at[h, s - 1], {"tile": place.along(1 - axis, p)})

    def ag2(h, s):
        axis, c1, c2, cols = line(h)
        p = (c1 + s) % SIDE
        return remote(total.at[c1, :, cols], total.at[c1, :, cols], ag2_send.at[h, s - 1], ag2_recv.at[h, s - 1],
                      {"tile": place.along(axis, p)})

    steps = range(1, SIDE)
    for h in (0, 1):
        for s in steps:
            rs1(h, s).start()
    for h in (0, 1):
        axis, c1, c2, cols = line(h)
        for s in steps:
            rs1(h, s).wait_recv()
        middle[h][...] = ((part[c1, :, cols] + land[h][0]) + (land[h][1] + land[h][2]))
        for s in steps:
            rs2(h, s).start()
    for h in (0, 1):
        axis, c1, c2, cols = line(h)
        for s in steps:
            rs2(h, s).wait_recv()
        strip_rows = pl.ds(pl.multiple_of(c2 * strip, strip), strip)
        own[h][...] = ((middle[h][strip_rows, :] + land2[h][0]) + (land2[h][1] + land2[h][2]))
        for s in steps:
            ag1(h, s).start()
        total[c1, strip_rows, cols] = own[h][...]
    for h in (0, 1):
        for s in steps:
            ag1(h, s).wait_recv()
        for s in steps:
            ag2(h, s).start()
    for h in (0, 1):
        for s in steps:
            ag2(h, s).wait_recv()
    for h in (0, 1):
        for s in steps:
            for copy in (rs1, rs2, ag1, ag2):
                copy(h, s).wait_send()

    for gather in sites:
        gather.forward()

    eye = lax.broadcasted_iota(jnp.int32, (NB, NB), 0) == lax.broadcasted_iota(jnp.int32, (NB, NB), 1)
    for i in range(blocks):
        o, e = i * NB, i * NB + NB
        src = view(total, 0) if i == 0 else s_ref.at[o:e, o:]
        factor_block(src[:, :NB] + jnp.where(eye, GRAM_SHIFT, 0.0), inv_ref)
        inv = inv_ref[...]
        q = f32_dot(r_ref[:, o:e], inv, (((1,), (1,)), ((), ())))
        q_ref[:, :, o:e] = q.reshape(legs, share, NB).astype(q_ref.dtype)
        if e == width:
            break
        upper = f32_dot(inv, src[:, NB:])
        r_ref[:, e:] = r_ref[:, e:] - f32_dot(q, upper)
        for k in range(i + 1, blocks):
            before = view(total, k)[...] if i == 0 else s_ref[k * NB:k * NB + NB, k * NB:]
            lo = (k - i - 1) * NB
            s_ref[k * NB:k * NB + NB, k * NB:] = before - f32_dot(upper[:, lo:lo + NB].T, upper[:, lo:])
    for gather in sites:
        gather.finish()


def front(site, sketch, phys_map):
    legs, share, width = site.shape
    packed = width + NB
    cut = NB * (width // NB // 2 + 1)
    sizes = (cut, packed - cut)
    strip = NB // SIDE
    f32 = jnp.float32
    three = pltpu.SemaphoreType.DMA((2, SIDE - 1))
    return pl.pallas_call(
        front_kernel,
        out_shape=(
            jax.ShapeDtypeStruct((legs, share, width), jnp.bfloat16),
            jax.ShapeDtypeStruct((legs, width, width), jnp.bfloat16),
        ),
        in_specs=[VMEM] * 3,
        out_specs=(VMEM, pl.BlockSpec(memory_space=pl.ANY)),
        scratch_shapes=[
            pltpu.VMEM((width, width), jnp.bfloat16),
            pltpu.VMEM((legs * share, width), f32),
            pltpu.VMEM((SIDE, NB, packed), f32),
            pltpu.VMEM((SIDE, NB, packed), f32),
            pltpu.VMEM((width, width), f32),
            pltpu.VMEM((NB, NB), f32),
            *[pltpu.VMEM((SIDE - 1, NB, size), f32) for size in sizes],
            *[pltpu.VMEM((NB, size), f32) for size in sizes],
            *[pltpu.VMEM((SIDE - 1, strip, size), f32) for size in sizes],
            *[pltpu.VMEM((strip, size), f32) for size in sizes],
            *LINE_SEMS,
            *LINE_SEMS,
            *[three] * 8,
            pltpu.SemaphoreType.DMA,
        ],
        compiler_params=pltpu.CompilerParams(collective_id=0, has_side_effects=True, vmem_limit_bytes=48 << 20),
    )(site, sketch, phys_map)


def site_kernel(cols, tiles, q_ref, edge_ref, ball_ref, kron_ref, close_ref, first_ref, out_ref, env_ref,
                ball, qall, lall, qt, x1, yh, yl, acc, osend, oall, tsend, across, arrived, stage, landed,
                gather_send, gather_recv, chain_send, chain_recv, spread_send, spread_recv,
                ball_sem, keep_sem, q1_send, q1_recv, q2_send, q2_recv, l1_send, l1_recv, l2_send, l2_recv,
                o_send, o_recv):
    place = Place()
    col = lax.axis_index("col")
    legs, share, width = q_ref.shape
    wide = width // SIDE
    first, last = col == 0, col == cols - 1
    barrier = pltpu.get_barrier_semaphore()
    fetch = pltpu.make_async_copy(ball_ref, ball, ball_sem)
    fetch.start()

    def greet(where):
        pl.semaphore_signal(barrier, inc=1, device_id=where, device_id_type=MESH)

    for s in range(1, tiles):
        greet({"tile": (place.tile + s) % tiles})
    for i in range(SIDE):
        greet({"col": (col + cols - 1) % cols, "tile": place.along(0, i)})
    pl.semaphore_wait(barrier, tiles - 1 + SIDE)

    def chunk(ref, index):
        return ref.at[:, :, pl.ds(pl.multiple_of(index * wide, wide), wide)]

    def slot(ref, tile, count=1):
        return ref.at[:, pl.ds(pl.multiple_of(tile * share, share), count * share), :]

    def q1(s):
        target = (place.y + s) % SIDE
        return remote(chunk(q_ref, target), slot(qall, place.tile), q1_send.at[s - 1], q1_recv.at[s - 1],
                      {"tile": place.along(1, target)})

    def q2(s, j):
        source = place.along(1, (place.y + SIDE - j) % SIDE)
        piece = chunk(q_ref, place.y) if j == 0 else slot(qall, source)
        return remote(piece, slot(qall, source), q2_send.at[s - 1, j], q2_recv.at[s - 1, j],
                      {"tile": place.along(0, (place.x + s) % SIDE)})

    def l1(ref, s, column):
        target = (place.x + s) % SIDE
        return remote(chunk(ref, target), slot(lall, place.tile), l1_send.at[s], l1_recv.at[s],
                      {"col": column, "tile": place.along(0, target)})

    def edge1(s):
        target = (place.x + s) % SIDE
        return remote(chunk(edge_ref, target), slot(lall, place.tile), l2_send.at[SIDE - 2 + s], l1_recv.at[s],
                      {"tile": place.along(0, target)})

    def l2(s):
        rows = slot(lall, place.y * SIDE, SIDE)
        return remote(rows, rows, l2_send.at[s - 1], l2_recv.at[s - 1],
                      {"tile": place.along(1, (place.y + s) % SIDE)})

    def edge_own():
        return pltpu.make_async_copy(chunk(edge_ref, place.x), slot(lall, place.tile), l1_recv.at[0])

    steps = range(1, SIDE)
    for s in steps:
        q1(s).start()

    @pl.when(jnp.logical_not(last))
    def _():
        for s in range(SIDE):
            l1(q_ref, s, col + 1).start()

    @pl.when(first)
    def _():
        edge_own().start()
        for s in steps:
            edge1(s).start()

    own = pltpu.make_async_copy(chunk(q_ref, place.y), slot(qall, place.tile), keep_sem)
    own.start()
    for s in steps:
        q2(s, 0).start()
    for j in steps:
        q1(j).wait_recv()
        for s in steps:
            q2(s, j).start()

    @pl.when(first)
    def _():
        edge_own().wait()
        for s in steps:
            edge1(s).wait_recv()

    @pl.when(jnp.logical_not(first))
    def _():
        for s in range(SIDE):
            l1(q_ref, s, col).wait_recv()

    for s in steps:
        l2(s).start()
    own.wait()
    for s in steps:
        for j in range(SIDE):
            q2(s, j).wait_recv()
    for r in range(legs):
        qt[r * wide:r * wide + wide, :] = qall[r].astype(jnp.float32).T.astype(jnp.bfloat16)
    fetch.wait()

    groups = wide // 16
    acc[...] = jnp.zeros_like(acc)

    @pl.loop(0, width // wide)
    def _(piece):
        lanes = pl.ds(pl.multiple_of(piece * wide, wide), wide)
        for u in range(legs):
            x1[:, u * wide:u * wide + wide] = jnp.dot(
                qt[...], ball[u, :, lanes], preferred_element_type=jnp.float32)

        @pl.loop(0, groups // 2)
        def _(pair):
            for g in (pair * 2, pair * 2 + 1):
                start = pl.multiple_of(g * 16, 16)
                stack = jnp.concatenate(
                    [x1[pl.ds(pl.multiple_of(r * wide + start, 16), 16), u * wide:u * wide + wide]
                     for u in range(legs) for r in range(legs)], axis=0)
                high = stack.astype(jnp.bfloat16)
                low = (stack - high.astype(jnp.float32)).astype(jnp.bfloat16)
                y = (jnp.dot(kron_ref[...], high, preferred_element_type=jnp.float32)
                     + jnp.dot(kron_ref[...], low, preferred_element_type=jnp.float32))
                high = y.astype(jnp.bfloat16)
                low = (y - high.astype(jnp.float32)).astype(jnp.bfloat16)
                rows = pl.ds(pl.multiple_of(g * 64, 64), 64)
                for l in range(legs):
                    yh[l, rows, :] = high[l * 64:l * 64 + 64]
                    yl[l, rows, :] = low[l * 64:l * 64 + 64]

        @pl.when(piece == 0)
        def _():
            for s in steps:
                l2(s).wait_recv()

        for l in range(legs):
            left = lall[l, lanes, :]
            term = (jnp.dot(yh[l], left, preferred_element_type=jnp.float32)
                    + jnp.dot(yl[l], left, preferred_element_type=jnp.float32))
            acc[...] = acc[...] + term

    def out(s):
        target = (place.x + s) % SIDE
        return remote(osend.at[pl.ds(pl.multiple_of(target * wide, wide), wide)],
                      oall.at[:, pl.ds(pl.multiple_of(place.x * wide, wide), wide)],
                      o_send.at[s - 1], o_recv.at[s - 1], {"tile": place.along(0, target)})

    owner = place.tile == OWNER
    others = [t for t in range(tiles) if t != OWNER]
    block = (pl.ds(pl.multiple_of(place.x * wide, wide), wide), pl.ds(pl.multiple_of(place.y * wide, wide), wide))

    def gather(slot):
        return remote(tsend, across.at[block], gather_send, gather_recv.at[slot], {"tile": OWNER})

    def spread(where):
        return remote(stage, landed, spread_send.at[where], spread_recv, {"tile": where})

    def chain(where):
        return remote(stage, arrived, chain_send, chain_recv, {"col": where})

    def scale_of(raw):
        squares = jnp.sum(raw * raw, axis=1, keepdims=True)
        return jnp.sqrt(jnp.float32(width)) / jnp.sqrt(squares + 1e-06)

    osend[...] = acc[...].astype(jnp.bfloat16)
    rows = []
    for g in range(groups):
        t = None
        for d in range(legs):
            lo = (g * legs + d) * 16
            term = osend[lo:lo + 16, :].astype(jnp.float32) * close_ref[0, d]
            t = term if t is None else t + term
        rows.append(t)
    transfer = jnp.concatenate(rows, axis=0).astype(jnp.bfloat16).astype(jnp.float32)
    tsend[...] = transfer.T.astype(jnp.bfloat16)

    @pl.when(jnp.logical_not(owner))
    def _():
        gather(place.tile).start()

    for s in steps:
        out(s).start()
    mine = pl.multiple_of(place.x * wide, wide)
    oall[:, pl.ds(mine, wide)] = osend[pl.ds(mine, wide), :]

    @pl.when(owner)
    def _():
        across[block] = tsend[...]
        for t in others:
            gather(t).wait_recv()

        @pl.when(first)
        def _():
            arrived[...] = first_ref[...]

        @pl.when(jnp.logical_not(first))
        def _():
            chain(col).wait_recv()

        raw = arrived[...]
        high = raw.astype(jnp.bfloat16).astype(jnp.float32)
        middle = (raw - high).astype(jnp.bfloat16).astype(jnp.float32)
        low = raw - high - middle
        row = lax.broadcasted_iota(jnp.int32, (8, width), 0)
        parts = jnp.where(row == 0, high, jnp.where(row == 1, middle, jnp.where(row == 2, low, 0.0)))
        product = jnp.dot(parts.astype(jnp.bfloat16), across[...], preferred_element_type=jnp.float32)
        scale = jnp.where(first, 1.0, scale_of(raw))
        stage[...] = jnp.sum(product, axis=0, keepdims=True) * scale

        @pl.when(jnp.logical_not(last))
        def _():
            chain(col + 1).start()

        for t in others:
            spread(t).start()
        weighted = stage[...]
        env_ref[...] = weighted * scale_of(weighted)

    for s in steps:
        out(s).wait_recv()
    out_ref[...] = oall[...]

    @pl.when(owner)
    def _():
        for t in others:
            spread(t).wait_send()

        @pl.when(jnp.logical_not(last))
        def _():
            chain(col + 1).wait_send()

    @pl.when(jnp.logical_not(owner))
    def _():
        spread(OWNER).wait_recv()
        weighted = landed[...]
        env_ref[...] = weighted * scale_of(weighted)
        gather(place.tile).wait_send()

    for s in steps:
        q1(s).wait_send()
        l2(s).wait_send()
        out(s).wait_send()
        for j in range(SIDE):
            q2(s, j).wait_send()

    @pl.when(first)
    def _():
        for s in steps:
            edge1(s).wait_send()

    @pl.when(jnp.logical_not(last))
    def _():
        for s in range(SIDE):
            l1(q_ref, s, col + 1).wait_send()


def new_site_of(basis, edge, whole_site, kron, closing, left_edge, cols, tiles):
    legs, share, width = basis.shape
    wide = width // SIDE
    bf16, f32 = jnp.bfloat16, jnp.float32
    dma = pltpu.SemaphoreType.DMA
    return pl.pallas_call(
        functools.partial(site_kernel, cols, tiles),
        out_shape=(
            jax.ShapeDtypeStruct((legs * share, width), bf16),
            jax.ShapeDtypeStruct((1, width), f32),
        ),
        in_specs=[VMEM, VMEM, pl.BlockSpec(memory_space=pl.ANY), VMEM, pl.BlockSpec(memory_space=pltpu.SMEM), VMEM],
        out_specs=(VMEM, VMEM),
        scratch_shapes=[
            pltpu.VMEM((legs, width, width), bf16),
            pltpu.VMEM((legs, width, wide), bf16),
            pltpu.VMEM((legs, width, wide), bf16),
            pltpu.VMEM((legs * wide, width), bf16),
            pltpu.VMEM((legs * wide, legs * wide), f32),
            pltpu.VMEM((legs, legs * wide, wide), bf16),
            pltpu.VMEM((legs, legs * wide, wide), bf16),
            pltpu.VMEM((legs * wide, wide), f32),
            pltpu.VMEM((legs * wide, wide), bf16),
            pltpu.VMEM((legs * share, width), bf16),
            pltpu.VMEM((wide, wide), bf16),
            pltpu.VMEM((width, width), bf16),
            pltpu.VMEM((1, width), f32),
            pltpu.VMEM((1, width), f32),
            pltpu.VMEM((1, width), f32),
            dma, dma((tiles,)), dma, dma, dma((tiles,)), dma,
            dma, dma,
            dma((SIDE - 1,)), dma((SIDE - 1,)),
            dma((SIDE - 1, SIDE)), dma((SIDE - 1, SIDE)),
            dma((SIDE,)), dma((SIDE,)),
            dma((2 * SIDE - 2,)), dma((SIDE - 1,)),
            dma((SIDE - 1,)), dma((SIDE - 1,)),
        ],
        compiler_params=pltpu.CompilerParams(collective_id=2, has_side_effects=True, vmem_limit_bytes=56 << 20),
    )(basis, edge, whole_site, kron, closing, left_edge.reshape(1, width))


def local(boundary, row_tensors, sketch_bond, sketch_phys, edge_factor, closing, left_edge):
    cols, tiles = lax.axis_size("col"), lax.axis_size("tile")
    share, legs, width = boundary.shape[1:]
    row_tensor = row_tensors[0]
    phys_map = jnp.einsum(
        "lurd,ldk->urk", row_tensor.astype(jnp.float32), sketch_phys[0].astype(jnp.float32), precision=HIGHEST
    )
    basis, whole_site = front(
        boundary[0].transpose(1, 0, 2), sketch_bond[0], phys_map.reshape(legs * legs, width))
    kron = jnp.einsum("lurd,st->ldsurt", row_tensor.astype(jnp.float32), jnp.eye(16, dtype=jnp.float32),
                      precision=HIGHEST)
    kron = kron.reshape(16 * legs * legs, 16 * legs * legs).astype(jnp.bfloat16)
    rows, env = new_site_of(
        basis, edge_factor.transpose(1, 0, 2), whole_site, kron, closing, left_edge, cols, tiles)
    new_site = rows.reshape(share // 16, legs, 16, width).transpose(0, 2, 1, 3).reshape(share, legs, width)
    env_local = lax.dynamic_slice(env, (0, lax.axis_index("tile") * share), (1, share))
    return (new_site[None], env_local)


def solution(mesh):
    in_specs = (
        P("col", "tile", None, None),
        P("col", None, None, None, None),
        P("col", "tile", None),
        P("col", None, None, None),
        P("tile", None, None),
        P("col", None),
        P(),
    )
    out_specs = (P("col", "tile", None, None), P("col", "tile"))
    return jax.shard_map(local, mesh=mesh, in_specs=in_specs, out_specs=out_specs, check_vma=False)
```

profile of v0, /device:TPU:229, one launch (start us, length us, event | category | flops | bytes accessed | tf_op | source)
XLA Modules:
  0.0 244.9 jit_solution(7896960220669244806)
XLA Ops:
  0.6 0.0 copy-start
  0.6 0.0 copy-start.3
  0.7 1.3 copy.20
  1.9 0.0 copy-done
  1.9 0.9 convolution_bitcast_fusion.phys_ref
  2.8 0.0 copy-start.2
  2.8 0.9 copy-done.2
  3.8 120.5 %shard_map.86 = (bf16[4,64,1024]{2,1,0:T(8,128)(2,1)S(1)}, bf16[4,1024,1024]{2,1,0:T(8,128)(2,1)}) custom-call(bf16[4,64,1024]{2,1,0:T(8,128)(2,1)S(1)} %bitcast.28, bf16[64,1024]{1,0:T(8,128)(2,1)S(1)} %bitcast.29, f32[16,1024]{1,0:T(8,128)S(1)} %convolution_bitcast_fusion.phys_ref), custom_call_target="tpu_custom_call" | custom-call | tf_op jit(solution)/shard_map/pallas_call | solution.py:307
  124.2 0.0 copy-start.1
  124.2 0.8 copy-done.1
  125.0 0.7 bitcast_convert_fusion
  125.7 0.2 copy.13
  126.0 0.4 fusion
  126.4 1.6 convert_element_type.13.kron_ref
  128.0 0.0 copy-done.3
  128.0 1.0 copy.19
  129.0 112.4 %shard_map.87 = (bf16[256,1024]{1,0:T(8,128)(2,1)}, f32[1,1024]{1,0:T(1,128)}) custom-call(bf16[4,64,1024]{2,1,0:T(8,128)(2,1)} %copy-done.1, bf16[4,64,1024]{2,1,0:T(8,128)(2,1)} %bitcast.30, bf16[4,1024,1024]{2,1,0:T(8,128)(2,1)} %get-tuple-element.7.ball_ref, bf16[256,256]{1,0:T(8,128)(2,1)} %convert_element_type.13.kron_ref, f32[1,4]{1,0:T(1,128)} %close_ref.1, ...), custom_call_target="tpu_custom_call" | custom-call | tf_op jit(solution)/shard_map/pallas_call | solution.py:597
  241.4 1.2 constant_dynamic-slice_fusion
  242.6 2.2 copy.14
  (1 shorter events, 0.0 us)
Async XLA Ops:
  0.6 1.3 copy-start
  0.6 127.4 %copy-start.3 = (bf16[64,4,1024]{2,1,0:T(4,128)(2,1)S(1)}, bf16[64,4,1024]{2,1,0:T(4,128)(2,1)}, u32[]{:S(2)}) copy-start(bf16[64,4,1024]{2,1,0:T(4,128)(2,1)} %param.11) | copy-start | bytes 1572868
  2.8 0.9 copy-start.2
  124.2 0.8 copy-start.1
where the time goes:
time: 245 us
  Pallas kernels  233 us (95%)
  local copies, waits for them, and re-layouts  9.27 us (4%)
    pallas_call x1, Pallas kernels, front(): pl.pallas_call(front_kernel, out_shape=(jax.ShapeDtypeStruct((legs, share...  120 us
    pallas_call x1, Pallas kernels, new_site_of(): pl.pallas_call(functools.partial(site_kernel, cols, tiles), out_shape=(ja...  112 us

commit v1 on v0

--- a/solution.py
+++ b/solution.py
@@ -141,19 +141,29 @@
 ]
 
 
-def front_kernel(b_ref, g_ref, phys_ref, q_ref, ball_ref, gall, r_ref, part, total, s_ref, inv_ref, *scratch):
-    land, middle, land2, own = scratch[:2], scratch[2:4], scratch[4:6], scratch[6:8]
-    sems = scratch[8:]
-    g_sems, b_sems = sems[0:4], sems[4:8]
-    rs1_send, rs1_recv, rs2_send, rs2_recv, ag1_send, ag1_recv, ag2_send, ag2_recv, here_sem = sems[8:]
+def kernel(cols, tiles, b_ref, g_ref, amat_ref, h_ref, edge_ref, close_ref, first_ref, out_ref, env_ref, *scratch):
+    (gall, r_ref, part, total, s_ref, inv_ref, kron_ref, phys_ref, q_ref, ball, qall, lall, qt, x1, yh, yl, acc, osend, oall,
+     tsend, across, arrived, stage, landed) = scratch[:24]
+    land, middle, land2, own = scratch[24:26], scratch[26:28], scratch[28:30], scratch[30:32]
+    g_sems, b_sems = scratch[32:36], scratch[36:40]
+    rs1_send, rs1_recv, rs2_send, rs2_recv, ag1_send, ag1_recv, ag2_send, ag2_recv, here_sem = scratch[40:49]
+    (gather_send, gather_recv, chain_send, chain_recv, spread_send, spread_recv, keep_sem, q1_send, q1_recv, q2_send, q2_recv,
+     l1_send, l1_recv, l2_send, l2_recv, o_send, o_recv) = scratch[49:]
     place = Place()
+    col = lax.axis_index("col")
     legs, share, width = b_ref.shape
+    wide = width // SIDE
+    first, last = col == 0, col == cols - 1
     barrier = pltpu.get_barrier_semaphore()
-    for axis in (0, 1):
-        for s in range(1, SIDE):
-            target = place.along(axis, (place.coordinate(axis) + s) % SIDE)
-            pl.semaphore_signal(barrier, inc=1, device_id={"tile": target}, device_id_type=MESH)
-    pl.semaphore_wait(barrier, 2 * (SIDE - 1))
+
+    def greet(where):
+        pl.semaphore_signal(barrier, inc=1, device_id=where, device_id_type=MESH)
+
+    for s in range(1, tiles):
+        greet({"tile": (place.tile + s) % tiles})
+    for i in range(SIDE):
+        greet({"col": (col + cols - 1) % cols, "tile": place.along(0, i)})
+    pl.semaphore_wait(barrier, tiles - 1 + SIDE)
 
     half = share // 2
     sketch = [
@@ -167,22 +177,82 @@
         gather.start()
     mine = pl.multiple_of(place.tile * share, share)
     gall[pl.ds(mine, share), :] = g_ref[...]
-    keep = pltpu.make_async_copy(b_ref, ball_ref.at[:, pl.ds(mine, share), :], here_sem)
+    keep = pltpu.make_async_copy(b_ref, ball.at[:, pl.ds(mine, share), :], here_sem)
     keep.start()
+    legs_sq = legs * legs
+    spread_rows = lax.broadcasted_iota(jnp.int32, (16 * legs_sq, legs_sq), 0) // 16
+    spread_cols = lax.broadcasted_iota(jnp.int32, (16 * legs_sq, legs_sq), 1)
+    repeat = (spread_rows == spread_cols).astype(jnp.float32)
+    mixed = f32_dot(f32_dot(repeat, amat_ref[...].T), repeat, (((1,), (1,)), ((), ())))
+    same = (lax.broadcasted_iota(jnp.int32, mixed.shape, 0) % 16) == (lax.broadcasted_iota(jnp.int32, mixed.shape, 1) % 16)
+    kron_ref[...] = jnp.where(same, mixed, 0.0).astype(jnp.bfloat16)
+    phys_ref[...] = f32_dot(
+        amat_ref[...], jnp.concatenate([h_ref[l].astype(jnp.float32) for l in range(legs)], axis=0))
     for gather in sketch:
         gather.forward()
     for gather in sketch:
         gather.finish()
 
+    def chunk(ref, index):
+        return ref.at[:, :, pl.ds(pl.multiple_of(index * wide, wide), wide)]
+
+    def slot(ref, tile, count=1):
+        return ref.at[:, pl.ds(pl.multiple_of(tile * share, share), count * share), :]
+
+    def q1(s):
+        target = (place.y + s) % SIDE
+        return remote(chunk(q_ref, target), slot(qall, place.tile), q1_send.at[s - 1], q1_recv.at[s - 1],
+                      {"tile": place.along(1, target)})
+
+    def q2(s, j):
+        source = place.along(1, (place.y + SIDE - j) % SIDE)
+        piece = chunk(q_ref, place.y) if j == 0 else slot(qall, source)
+        return remote(piece, slot(qall, source), q2_send.at[s - 1, j], q2_recv.at[s - 1, j],
+                      {"tile": place.along(0, (place.x + s) % SIDE)})
+
+    def l1(ref, s, column):
+        target = (place.x + s) % SIDE
+        return remote(chunk(ref, target), slot(lall, place.tile), l1_send.at[s], l1_recv.at[s],
+                      {"col": column, "tile": place.along(0, target)})
+
+    def edge1(s):
+        target = (place.x + s) % SIDE
+        return remote(chunk(edge_ref, target), slot(lall, place.tile), l2_send.at[SIDE - 2 + s], l1_recv.at[s],
+                      {"tile": place.along(0, target)})
+
+    def l2(s):
+        rows = slot(lall, place.y * SIDE, SIDE)
+        return remote(rows, rows, l2_send.at[s - 1], l2_recv.at[s - 1],
+                      {"tile": place.along(1, (place.y + s) % SIDE)})
+
+    def edge_own():
+        return pltpu.make_async_copy(chunk(edge_ref, place.x), slot(lall, place.tile), l1_recv.at[0])
+
+    def send_chunk(index):
+        step = (index - place.y + SIDE) % SIDE
+
+        @pl.when(step > 0)
+        def _():
+            q1(step).start()
+
+        @pl.when(jnp.logical_not(last))
+        def _():
+            l1(q_ref, (index - place.x + SIDE) % SIDE, col + 1).start()
+
+    @pl.when(first)
+    def _():
+        edge_own().start()
+        for s in range(1, SIDE):
+            edge1(s).start()
+
     two = legs // 2
     sites = [
         LineGather(
             place, h, b_ref.at[h * two:h * two + two],
-            lambda tile, h=h: ball_ref.at[h * two:h * two + two, pl.ds(pl.multiple_of(tile * share, share), share), :],
+            lambda tile, h=h: ball.at[h * two:h * two + two, pl.ds(pl.multiple_of(tile * share, share), share), :],
             [x.at[h] for x in b_sems])
         for h in (0, 1)
     ]
-    keep.wait()
     for gather in sites:
         gather.start()
 
@@ -284,6 +354,8 @@
         inv = inv_ref[...]
         q = f32_dot(r_ref[:, o:e], inv, (((1,), (1,)), ((), ())))
         q_ref[:, :, o:e] = q.reshape(legs, share, NB).astype(q_ref.dtype)
+        if e % wide == 0:
+            send_chunk(e // wide - 1)
         if e == width:
             break
         upper = f32_dot(inv, src[:, NB:])
@@ -292,121 +364,9 @@
             before = view(total, k)[...] if i == 0 else s_ref[k * NB:k * NB + NB, k * NB:]
             lo = (k - i - 1) * NB
             s_ref[k * NB:k * NB + NB, k * NB:] = before - f32_dot(upper[:, lo:lo + NB].T, upper[:, lo:])
-    for gather in sites:
-        gather.finish()
-
-
-def front(site, sketch, phys_map):
-    legs, share, width = site.shape
-    packed = width + NB
-    cut = NB * (width // NB // 2 + 1)
-    sizes = (cut, packed - cut)
-    strip = NB // SIDE
-    f32 = jnp.float32
-    three = pltpu.SemaphoreType.DMA((2, SIDE - 1))
-    return pl.pallas_call(
-        front_kernel,
-        out_shape=(
-            jax.ShapeDtypeStruct((legs, share, width), jnp.bfloat16),
-            jax.ShapeDtypeStruct((legs, width, width), jnp.bfloat16),
-        ),
-        in_specs=[VMEM] * 3,
-        out_specs=(VMEM, pl.BlockSpec(memory_space=pl.ANY)),
-        scratch_shapes=[
-            pltpu.VMEM((width, width), jnp.bfloat16),
-            pltpu.VMEM((legs * share, width), f32),
-            pltpu.VMEM((SIDE, NB, packed), f32),
-            pltpu.VMEM((SIDE, NB, packed), f32),
-            pltpu.VMEM((width, width), f32),
-            pltpu.VMEM((NB, NB), f32),
-            *[pltpu.VMEM((SIDE - 1, NB, size), f32) for size in sizes],
-            *[pltpu.VMEM((NB, size), f32) for size in sizes],
-            *[pltpu.VMEM((SIDE - 1, strip, size), f32) for size in sizes],
-            *[pltpu.VMEM((strip, size), f32) for size in sizes],
-            *LINE_SEMS,
-            *LINE_SEMS,
-            *[three] * 8,
-            pltpu.SemaphoreType.DMA,
-        ],
-        compiler_params=pltpu.CompilerParams(collective_id=0, has_side_effects=True, vmem_limit_bytes=48 << 20),
-    )(site, sketch, phys_map)
-
-
-def site_kernel(cols, tiles, q_ref, edge_ref, ball_ref, kron_ref, close_ref, first_ref, out_ref, env_ref,
-                ball, qall, lall, qt, x1, yh, yl, acc, osend, oall, tsend, across, arrived, stage, landed,
-                gather_send, gather_recv, chain_send, chain_recv, spread_send, spread_recv,
-                ball_sem, keep_sem, q1_send, q1_recv, q2_send, q2_recv, l1_send, l1_recv, l2_send, l2_recv,
-                o_send, o_recv):
-    place = Place()
-    col = lax.axis_index("col")
-    legs, share, width = q_ref.shape
-    wide = width // SIDE
-    first, last = col == 0, col == cols - 1
-    barrier = pltpu.get_barrier_semaphore()
-    fetch = pltpu.make_async_copy(ball_ref, ball, ball_sem)
-    fetch.start()
-
-    def greet(where):
-        pl.semaphore_signal(barrier, inc=1, device_id=where, device_id_type=MESH)
-
-    for s in range(1, tiles):
-        greet({"tile": (place.tile + s) % tiles})
-    for i in range(SIDE):
-        greet({"col": (col + cols - 1) % cols, "tile": place.along(0, i)})
-    pl.semaphore_wait(barrier, tiles - 1 + SIDE)
-
-    def chunk(ref, index):
-        return ref.at[:, :, pl.ds(pl.multiple_of(index * wide, wide), wide)]
-
-    def slot(ref, tile, count=1):
-        return ref.at[:, pl.ds(pl.multiple_of(tile * share, share), count * share), :]
-
-    def q1(s):
-        target = (place.y + s) % SIDE
-        return remote(chunk(q_ref, target), slot(qall, place.tile), q1_send.at[s - 1], q1_recv.at[s - 1],
-                      {"tile": place.along(1, target)})
-
-    def q2(s, j):
-        source = place.along(1, (place.y + SIDE - j) % SIDE)
-        piece = chunk(q_ref, place.y) if j == 0 else slot(qall, source)
-        return remote(piece, slot(qall, source), q2_send.at[s - 1, j], q2_recv.at[s - 1, j],
-                      {"tile": place.along(0, (place.x + s) % SIDE)})
-
-    def l1(ref, s, column):
-        target = (place.x + s) % SIDE
-        return remote(chunk(ref, target), slot(lall, place.tile), l1_send.at[s], l1_recv.at[s],
-                      {"col": column, "tile": place.along(0, target)})
-
-    def edge1(s):
-        target = (place.x + s) % SIDE
-        return remote(chunk(edge_ref, target), slot(lall, place.tile), l2_send.at[SIDE - 2 + s], l1_recv.at[s],
-                      {"tile": place.along(0, target)})
-
-    def l2(s):
-        rows = slot(lall, place.y * SIDE, SIDE)
-        return remote(rows, rows, l2_send.at[s - 1], l2_recv.at[s - 1],
-                      {"tile": place.along(1, (place.y + s) % SIDE)})
-
-    def edge_own():
-        return pltpu.make_async_copy(chunk(edge_ref, place.x), slot(lall, place.tile), l1_recv.at[0])
-
-    steps = range(1, SIDE)
-    for s in steps:
-        q1(s).start()
-
-    @pl.when(jnp.logical_not(last))
-    def _():
-        for s in range(SIDE):
-            l1(q_ref, s, col + 1).start()
-
-    @pl.when(first)
-    def _():
-        edge_own().start()
-        for s in steps:
-            edge1(s).start()
-
-    own = pltpu.make_async_copy(chunk(q_ref, place.y), slot(qall, place.tile), keep_sem)
-    own.start()
+
+    keep_q = pltpu.make_async_copy(chunk(q_ref, place.y), slot(qall, place.tile), keep_sem)
+    keep_q.start()
     for s in steps:
         q2(s, 0).start()
     for j in steps:
@@ -427,13 +387,15 @@
 
     for s in steps:
         l2(s).start()
-    own.wait()
+    keep_q.wait()
     for s in steps:
         for j in range(SIDE):
             q2(s, j).wait_recv()
     for r in range(legs):
         qt[r * wide:r * wide + wide, :] = qall[r].astype(jnp.float32).T.astype(jnp.bfloat16)
-    fetch.wait()
+    keep.wait()
+    for gather in sites:
+        gather.finish()
 
     groups = wide // 16
     acc[...] = jnp.zeros_like(acc)
@@ -589,61 +551,77 @@
             l1(q_ref, s, col + 1).wait_send()
 
 
-def new_site_of(basis, edge, whole_site, kron, closing, left_edge, cols, tiles):
-    legs, share, width = basis.shape
+def absorb(site, sketch, amat, phys, edge, closing, left_edge, cols, tiles):
+    legs, share, width = site.shape
     wide = width // SIDE
+    packed = width + NB
+    cut = NB * (width // NB // 2 + 1)
+    sizes = (cut, packed - cut)
+    strip = NB // SIDE
     bf16, f32 = jnp.bfloat16, jnp.float32
     dma = pltpu.SemaphoreType.DMA
+    three = dma((2, SIDE - 1))
+    vmem = pltpu.VMEM
     return pl.pallas_call(
-        functools.partial(site_kernel, cols, tiles),
+        functools.partial(kernel, cols, tiles),
         out_shape=(
             jax.ShapeDtypeStruct((legs * share, width), bf16),
             jax.ShapeDtypeStruct((1, width), f32),
         ),
-        in_specs=[VMEM, VMEM, pl.BlockSpec(memory_space=pl.ANY), VMEM, pl.BlockSpec(memory_space=pltpu.SMEM), VMEM],
+        in_specs=[VMEM] * 5 + [pl.BlockSpec(memory_space=pltpu.SMEM), VMEM],
         out_specs=(VMEM, VMEM),
         scratch_shapes=[
-            pltpu.VMEM((legs, width, width), bf16),
-            pltpu.VMEM((legs, width, wide), bf16),
-            pltpu.VMEM((legs, width, wide), bf16),
-            pltpu.VMEM((legs * wide, width), bf16),
-            pltpu.VMEM((legs * wide, legs * wide), f32),
-            pltpu.VMEM((legs, legs * wide, wide), bf16),
-            pltpu.VMEM((legs, legs * wide, wide), bf16),
-            pltpu.VMEM((legs * wide, wide), f32),
-            pltpu.VMEM((legs * wide, wide), bf16),
-            pltpu.VMEM((legs * share, width), bf16),
-            pltpu.VMEM((wide, wide), bf16),
-            pltpu.VMEM((width, width), bf16),
-            pltpu.VMEM((1, width), f32),
-            pltpu.VMEM((1, width), f32),
-            pltpu.VMEM((1, width), f32),
+            vmem((width, width), bf16),
+            vmem((legs * share, width), f32),
+            vmem((SIDE, NB, packed), f32),
+            vmem((SIDE, NB, packed), f32),
+            vmem((width, width), f32),
+            vmem((NB, NB), f32),
+            vmem((16 * legs * legs, 16 * legs * legs), bf16),
+            vmem((legs * legs, width), f32),
+            vmem((legs, share, width), bf16),
+            vmem((legs, width, width), bf16),
+            vmem((legs, width, wide), bf16),
+            vmem((legs, width, wide), bf16),
+            vmem((legs * wide, width), bf16),
+            vmem((legs * wide, legs * wide), f32),
+            vmem((legs, legs * wide, wide), bf16),
+            vmem((legs, legs * wide, wide), bf16),
+            vmem((legs * wide, wide), f32),
+            vmem((legs * wide, wide), bf16),
+            vmem((legs * share, width), bf16),
+            vmem((wide, wide), bf16),
+            vmem((width, width), bf16),
+            vmem((1, width), f32),
+            vmem((1, width), f32),
+            vmem((1, width), f32),
+            *[vmem((SIDE - 1, NB, size), f32) for size in sizes],
+            *[vmem((NB, size), f32) for size in sizes],
+            *[vmem((SIDE - 1, strip, size), f32) for size in sizes],
+            *[vmem((strip, size), f32) for size in sizes],
+            *LINE_SEMS,
+            *LINE_SEMS,
+            *[three] * 8,
+            dma,
             dma, dma((tiles,)), dma, dma, dma((tiles,)), dma,
-            dma, dma,
+            dma,
             dma((SIDE - 1,)), dma((SIDE - 1,)),
             dma((SIDE - 1, SIDE)), dma((SIDE - 1, SIDE)),
             dma((SIDE,)), dma((SIDE,)),
             dma((2 * SIDE - 2,)), dma((SIDE - 1,)),
             dma((SIDE - 1,)), dma((SIDE - 1,)),
         ],
-        compiler_params=pltpu.CompilerParams(collective_id=2, has_side_effects=True, vmem_limit_bytes=56 << 20),
-    )(basis, edge, whole_site, kron, closing, left_edge.reshape(1, width))
+        compiler_params=pltpu.CompilerParams(collective_id=0, has_side_effects=True, vmem_limit_bytes=62 << 20),
+    )(site, sketch, amat, phys, edge, closing, left_edge.reshape(1, width))
 
 
 def local(boundary, row_tensors, sketch_bond, sketch_phys, edge_factor, closing, left_edge):
     cols, tiles = lax.axis_size("col"), lax.axis_size("tile")
     share, legs, width = boundary.shape[1:]
-    row_tensor = row_tensors[0]
-    phys_map = jnp.einsum(
-        "lurd,ldk->urk", row_tensor.astype(jnp.float32), sketch_phys[0].astype(jnp.float32), precision=HIGHEST
-    )
-    basis, whole_site = front(
-        boundary[0].transpose(1, 0, 2), sketch_bond[0], phys_map.reshape(legs * legs, width))
-    kron = jnp.einsum("lurd,st->ldsurt", row_tensor.astype(jnp.float32), jnp.eye(16, dtype=jnp.float32),
-                      precision=HIGHEST)
-    kron = kron.reshape(16 * legs * legs, 16 * legs * legs).astype(jnp.bfloat16)
-    rows, env = new_site_of(
-        basis, edge_factor.transpose(1, 0, 2), whole_site, kron, closing, left_edge, cols, tiles)
+    amat = row_tensors[0].astype(jnp.float32).transpose(1, 2, 0, 3).reshape(legs * legs, legs * legs)
+    rows, env = absorb(
+        boundary[0].transpose(1, 0, 2), sketch_bond[0], amat, sketch_phys[0], edge_factor.transpose(1, 0, 2),
+        closing, left_edge, cols, tiles)
     new_site = rows.reshape(share // 16, legs, 16, width).transpose(0, 2, 1, 3).reshape(share, legs, width)
     env_local = lax.dynamic_slice(env, (0, lax.axis_index("tile") * share), (1, share))
     return (new_site[None], env_local)

time: 245 us -> 240 us (0.980)
    pallas_call x2 -> x1, Pallas kernels: 233 us -> 232 us  [absorb(): pl.pallas_call(functools.partial(kernel, cols, tiles), out_shape=(jax.Sha...]
where the time goes in v1:
time: 240 us
  Pallas kernels  232 us (97%)
  local copies, waits for them, and re-layouts  7.2 us (3%)
    pallas_call x1, Pallas kernels, absorb(): pl.pallas_call(functools.partial(kernel, cols, tiles), out_shape=(jax.Sha...  232 us

profile of v1, /device:TPU:229, one launch (start us, length us, event | category | flops | bytes accessed | tf_op | source)
XLA Modules:
  0.0 240.0 jit_solution(7849552866906777159)
XLA Ops:
  0.6 0.0 copy-start.1
  0.6 0.0 copy-start
  0.6 2.1 copy.16
  2.7 0.0 copy-done.1
  2.7 0.7 reshape.22.amat_ref
  3.4 0.0 copy-done
  3.4 1.0 copy.15
  4.4 232.2 %shard_map.86 = (bf16[256,1024]{1,0:T(8,128)(2,1)}, f32[1,1024]{1,0:T(1,128)}) custom-call(bf16[4,64,1024]{2,1,0:T(8,128)(2,1)} %bitcast.20, bf16[64,1024]{1,0:T(8,128)(2,1)} %bitcast.24, f32[16,16]{1,0:T(8,128)} %reshape.22.amat_ref, bf16[4,4,1024]{2,1,0:T(4,128)(2,1)} %bitcast.25, bf16[4,64,1024]{2,1,0:T(8,128)(2,1)} %bitcast.21, f32[1,4]{1,0:T(1,128)} %close_ref.1, ...), custom_call_target="tpu_custom_call" | custom-call | tf_op jit(solution)/shard_map/pallas_call | solution.py:565
  236.5 2.2 copy.12
  238.8 1.2 constant_dynamic-slice_fusion
  (2 shorter events, 0.0 us)
Async XLA Ops:
  0.6 2.1 copy-start.1
  0.6 2.8 %copy-start = (bf16[64,4,1024]{2,1,0:T(4,128)(2,1)S(1)}, bf16[64,4,1024]{2,1,0:T(4,128)(2,1)}, u32[]{:S(2)}) copy-start(bf16[64,4,1024]{2,1,0:T(4,128)(2,1)} %param.11) | copy-start | bytes 1572868

commit v2 on v1

--- a/solution.py
+++ b/solution.py
@@ -275,9 +275,6 @@
         return ref.at[i if i < pairs else blocks - 1 - i, :, lo:lo + (blocks - i) * NB]
 
     flipped = r_ref[...].T
-    for i in range(blocks):
-        view(part, i)[...] = f32_dot(flipped[i * NB:i * NB + NB, :], r_ref[:, i * NB:])
-
     strip = NB // SIDE
 
     def line(h):
@@ -311,9 +308,19 @@
                       {"tile": place.along(axis, p)})
 
     steps = range(1, SIDE)
-    for h in (0, 1):
-        for s in steps:
-            rs1(h, s).start()
+
+    def send_pair(h, pair):
+        step = (pair - place.coordinate(h) + SIDE) % SIDE
+
+        @pl.when(step > 0)
+        def _():
+            rs1(h, step).start()
+
+    for pair in range(pairs):
+        for i in (pair, blocks - 1 - pair):
+            view(part, i)[...] = f32_dot(flipped[i * NB:i * NB + NB, :], r_ref[:, i * NB:])
+        for h in (0, 1):
+            send_pair(h, pair)
     for h in (0, 1):
         axis, c1, c2, cols = line(h)
         for s in steps:
@@ -391,50 +398,15 @@
     for s in steps:
         for j in range(SIDE):
             q2(s, j).wait_recv()
+    part_k = wide // 2
     for r in range(legs):
-        qt[r * wide:r * wide + wide, :] = qall[r].astype(jnp.float32).T.astype(jnp.bfloat16)
+        turned = qall[r].astype(jnp.float32).T.astype(jnp.bfloat16)
+        for h in (0, 1):
+            lo = (h * legs + r) * part_k
+            qt[lo:lo + part_k, :] = turned[h * part_k:h * part_k + part_k]
     keep.wait()
     for gather in sites:
         gather.finish()
-
-    groups = wide // 16
-    acc[...] = jnp.zeros_like(acc)
-
-    @pl.loop(0, width // wide)
-    def _(piece):
-        lanes = pl.ds(pl.multiple_of(piece * wide, wide), wide)
-        for u in range(legs):
-            x1[:, u * wide:u * wide + wide] = jnp.dot(
-                qt[...], ball[u, :, lanes], preferred_element_type=jnp.float32)
-
-        @pl.loop(0, groups // 2)
-        def _(pair):
-            for g in (pair * 2, pair * 2 + 1):
-                start = pl.multiple_of(g * 16, 16)
-                stack = jnp.concatenate(
-                    [x1[pl.ds(pl.multiple_of(r * wide + start, 16), 16), u * wide:u * wide + wide]
-                     for u in range(legs) for r in range(legs)], axis=0)
-                high = stack.astype(jnp.bfloat16)
-                low = (stack - high.astype(jnp.float32)).astype(jnp.bfloat16)
-                y = (jnp.dot(kron_ref[...], high, preferred_element_type=jnp.float32)
-                     + jnp.dot(kron_ref[...], low, preferred_element_type=jnp.float32))
-                high = y.astype(jnp.bfloat16)
-                low = (y - high.astype(jnp.float32)).astype(jnp.bfloat16)
-                rows = pl.ds(pl.multiple_of(g * 64, 64), 64)
-                for l in range(legs):
-                    yh[l, rows, :] = high[l * 64:l * 64 + 64]
-                    yl[l, rows, :] = low[l * 64:l * 64 + 64]
-
-        @pl.when(piece == 0)
-        def _():
-            for s in steps:
-                l2(s).wait_recv()
-
-        for l in range(legs):
-            left = lall[l, lanes, :]
-            term = (jnp.dot(yh[l], left, preferred_element_type=jnp.float32)
-                    + jnp.dot(yl[l], left, preferred_element_type=jnp.float32))
-            acc[...] = acc[...] + term
 
     def out(s):
         target = (place.x + s) % SIDE
@@ -444,10 +416,13 @@
 
     owner = place.tile == OWNER
     others = [t for t in range(tiles) if t != OWNER]
-    block = (pl.ds(pl.multiple_of(place.x * wide, wide), wide), pl.ds(pl.multiple_of(place.y * wide, wide), wide))
-
-    def gather(slot):
-        return remote(tsend, across.at[block], gather_send, gather_recv.at[slot], {"tile": OWNER})
+
+    def block(h):
+        return (pl.ds(pl.multiple_of(place.x * wide, wide), wide),
+                pl.ds(pl.multiple_of(place.y * wide + h * part_k, part_k), part_k))
+
+    def gather(h, slot):
+        return remote(tsend.at[h], across.at[block(h)], gather_send.at[h], gather_recv.at[h, slot], {"tile": OWNER})
 
     def spread(where):
         return remote(stage, landed, spread_send.at[where], spread_recv, {"tile": where})
@@ -459,21 +434,64 @@
         squares = jnp.sum(raw * raw, axis=1, keepdims=True)
         return jnp.sqrt(jnp.float32(width)) / jnp.sqrt(squares + 1e-06)
 
-    osend[...] = acc[...].astype(jnp.bfloat16)
-    rows = []
-    for g in range(groups):
-        t = None
-        for d in range(legs):
-            lo = (g * legs + d) * 16
-            term = osend[lo:lo + 16, :].astype(jnp.float32) * close_ref[0, d]
-            t = term if t is None else t + term
-        rows.append(t)
-    transfer = jnp.concatenate(rows, axis=0).astype(jnp.bfloat16).astype(jnp.float32)
-    tsend[...] = transfer.T.astype(jnp.bfloat16)
-
-    @pl.when(jnp.logical_not(owner))
-    def _():
-        gather(place.tile).start()
+    groups = part_k // 16
+    unroll = 4
+    for h in (0, 1):
+        acc[...] = jnp.zeros_like(acc)
+        base = h * legs * part_k
+
+        @pl.loop(0, width // wide)
+        def _(piece):
+            lanes = pl.ds(pl.multiple_of(piece * wide, wide), wide)
+            for u in range(legs):
+                x1[:, u * wide:u * wide + wide] = jnp.dot(
+                    qt[base:base + legs * part_k, :], ball[u, :, lanes], preferred_element_type=jnp.float32)
+
+            @pl.loop(0, groups // unroll)
+            def _(some):
+                for g in [some * unroll + k for k in range(unroll)]:
+                    start = pl.multiple_of(g * 16, 16)
+                    stack = jnp.concatenate(
+                        [x1[pl.ds(pl.multiple_of(r * part_k + start, 16), 16), u * wide:u * wide + wide]
+                         for u in range(legs) for r in range(legs)], axis=0)
+                    high = stack.astype(jnp.bfloat16)
+                    low = (stack - high.astype(jnp.float32)).astype(jnp.bfloat16)
+                    y = (jnp.dot(kron_ref[...], high, preferred_element_type=jnp.float32)
+                         + jnp.dot(kron_ref[...], low, preferred_element_type=jnp.float32))
+                    high = y.astype(jnp.bfloat16)
+                    low = (y - high.astype(jnp.float32)).astype(jnp.bfloat16)
+                    rows = pl.ds(pl.multiple_of(g * 64, 64), 64)
+                    for l in range(legs):
+                        yh[l, rows, :] = high[l * 64:l * 64 + 64]
+                        yl[l, rows, :] = low[l * 64:l * 64 + 64]
+
+            if h == 0:
+                @pl.when(piece == 0)
+                def _():
+                    for s in steps:
+                        l2(s).wait_recv()
+
+            for l in range(legs):
+                left = lall[l, lanes, :]
+                term = (jnp.dot(yh[l], left, preferred_element_type=jnp.float32)
+                        + jnp.dot(yl[l], left, preferred_element_type=jnp.float32))
+                acc[...] = acc[...] + term
+
+        osend[base:base + legs * part_k, :] = acc[...].astype(jnp.bfloat16)
+        strips = []
+        for g in range(groups):
+            t = None
+            for d in range(legs):
+                lo = base + (g * legs + d) * 16
+                term = osend[lo:lo + 16, :].astype(jnp.float32) * close_ref[0, d]
+                t = term if t is None else t + term
+            strips.append(t)
+        transfer = jnp.concatenate(strips, axis=0).astype(jnp.bfloat16).astype(jnp.float32)
+        tsend[h] = transfer.T.astype(jnp.bfloat16)
+
+        @pl.when(jnp.logical_not(owner))
+        def _():
+            gather(h, place.tile).start()
 
     for s in steps:
         out(s).start()
@@ -482,9 +500,10 @@
 
     @pl.when(owner)
     def _():
-        across[block] = tsend[...]
-        for t in others:
-            gather(t).wait_recv()
+        for h in (0, 1):
+            across[block(h)] = tsend[h]
+            for t in others:
+                gather(h, t).wait_recv()
 
         @pl.when(first)
         def _():
@@ -531,7 +550,8 @@
         spread(OWNER).wait_recv()
         weighted = landed[...]
         env_ref[...] = weighted * scale_of(weighted)
-        gather(place.tile).wait_send()
+        for h in (0, 1):
+            gather(h, place.tile).wait_send()
 
     for s in steps:
         q1(s).wait_send()
@@ -584,13 +604,13 @@
             vmem((legs, width, wide), bf16),
             vmem((legs, width, wide), bf16),
             vmem((legs * wide, width), bf16),
-            vmem((legs * wide, legs * wide), f32),
-            vmem((legs, legs * wide, wide), bf16),
-            vmem((legs, legs * wide, wide), bf16),
-            vmem((legs * wide, wide), f32),
+            vmem((legs * wide // 2, legs * wide), f32),
+            vmem((legs, legs * wide // 2, wide), bf16),
+            vmem((legs, legs * wide // 2, wide), bf16),
+            vmem((legs * wide // 2, wide), f32),
             vmem((legs * wide, wide), bf16),
             vmem((legs * share, width), bf16),
-            vmem((wide, wide), bf16),
+            vmem((2, wide, wide // 2), bf16),
             vmem((width, width), bf16),
             vmem((1, width), f32),
             vmem((1, width), f32),
@@ -603,7 +623,7 @@
             *LINE_SEMS,
             *[three] * 8,
             dma,
-            dma, dma((tiles,)), dma, dma, dma((tiles,)), dma,
+            dma((2,)), dma((2, tiles)), dma, dma, dma((tiles,)), dma,
             dma,
             dma((SIDE - 1,)), dma((SIDE - 1,)),
             dma((SIDE - 1, SIDE)), dma((SIDE - 1, SIDE)),

time: 240 us -> 234 us (0.975)
  Pallas kernels: 232 us -> 226 us
    pallas_call x1, Pallas kernels: 232 us -> 226 us  [absorb(): pl.pallas_call(functools.partial(kernel, cols, tiles), out_shape=(jax.Sha...]
where the time goes in v2:
time: 234 us
  Pallas kernels  226 us (97%)
  local copies, waits for them, and re-layouts  7.2 us (3%)
    pallas_call x1, Pallas kernels, absorb(): pl.pallas_call(functools.partial(kernel, cols, tiles), out_shape=(jax.Sha...  226 us

profile of v2, /device:TPU:229, one launch (start us, length us, event | category | flops | bytes accessed | tf_op | source)
XLA Modules:
  0.0 234.0 jit_solution(16905377005788337511)
XLA Ops:
  0.6 0.0 copy-start.1
  0.6 0.0 copy-start
  0.6 2.1 copy.16
  2.7 0.0 copy-done.1
  2.7 0.7 reshape.22.amat_ref
  3.4 0.0 copy-done
  3.4 1.0 copy.15
  4.4 226.1 %shard_map.86 = (bf16[256,1024]{1,0:T(8,128)(2,1)}, f32[1,1024]{1,0:T(1,128)}) custom-call(bf16[4,64,1024]{2,1,0:T(8,128)(2,1)} %bitcast.20, bf16[64,1024]{1,0:T(8,128)(2,1)} %bitcast.24, f32[16,16]{1,0:T(8,128)} %reshape.22.amat_ref, bf16[4,4,1024]{2,1,0:T(4,128)(2,1)} %bitcast.25, bf16[4,64,1024]{2,1,0:T(8,128)(2,1)} %bitcast.21, f32[1,4]{1,0:T(1,128)} %close_ref.1, ...), custom_call_target="tpu_custom_call" | custom-call | tf_op jit(solution)/shard_map/pallas_call | solution.py:585
  230.5 2.2 copy.12
  232.7 1.2 constant_dynamic-slice_fusion
  (2 shorter events, 0.0 us)
Async XLA Ops:
  0.6 2.1 copy-start.1
  0.6 2.8 %copy-start = (bf16[64,4,1024]{2,1,0:T(4,128)(2,1)S(1)}, bf16[64,4,1024]{2,1,0:T(4,128)(2,1)}, u32[]{:S(2)}) copy-start(bf16[64,4,1024]{2,1,0:T(4,128)(2,1)} %param.11) | copy-start | bytes 1572868

commit v3 on v2

--- a/solution.py
+++ b/solution.py
@@ -148,7 +148,7 @@
     g_sems, b_sems = scratch[32:36], scratch[36:40]
     rs1_send, rs1_recv, rs2_send, rs2_recv, ag1_send, ag1_recv, ag2_send, ag2_recv, here_sem = scratch[40:49]
     (gather_send, gather_recv, chain_send, chain_recv, spread_send, spread_recv, keep_sem, q1_send, q1_recv, q2_send, q2_recv,
-     l1_send, l1_recv, l2_send, l2_recv, o_send, o_recv) = scratch[49:]
+     l1_send, l1_recv, l2_send, l2_recv, o_send, o_recv, r_send, r_recv) = scratch[49:]
     place = Place()
     col = lax.axis_index("col")
     legs, share, width = b_ref.shape
@@ -161,9 +161,15 @@
 
     for s in range(1, tiles):
         greet({"tile": (place.tile + s) % tiles})
-    for i in range(SIDE):
-        greet({"col": (col + cols - 1) % cols, "tile": place.along(0, i)})
-    pl.semaphore_wait(barrier, tiles - 1 + SIDE)
+    greet({"col": (col + cols - 1) % cols})
+    pl.semaphore_wait(barrier, tiles)
+    odd = col % 2
+    k_step, c_step = SIDE - (SIDE - 1) * odd, 1 + (SIDE - 1) * odd
+    k_index = place.y + (place.x - place.y) * odd
+    c_index = place.x + (place.y - place.x) * odd
+
+    def tile_of(k_block, c_block):
+        return k_block * k_step + c_block * c_step
 
     half = share // 2
     sketch = [
@@ -200,24 +206,29 @@
         return ref.at[:, pl.ds(pl.multiple_of(tile * share, share), count * share), :]
 
     def q1(s):
-        target = (place.y + s) % SIDE
+        target = (k_index + s) % SIDE
         return remote(chunk(q_ref, target), slot(qall, place.tile), q1_send.at[s - 1], q1_recv.at[s - 1],
-                      {"tile": place.along(1, target)})
+                      {"tile": tile_of(target, c_index)})
 
     def q2(s, j):
-        source = place.along(1, (place.y + SIDE - j) % SIDE)
-        piece = chunk(q_ref, place.y) if j == 0 else slot(qall, source)
+        source = tile_of((k_index + SIDE - j) % SIDE, c_index)
+        piece = chunk(q_ref, k_index) if j == 0 else slot(qall, source)
         return remote(piece, slot(qall, source), q2_send.at[s - 1, j], q2_recv.at[s - 1, j],
-                      {"tile": place.along(0, (place.x + s) % SIDE)})
-
-    def l1(ref, s, column):
-        target = (place.x + s) % SIDE
-        return remote(chunk(ref, target), slot(lall, place.tile), l1_send.at[s], l1_recv.at[s],
-                      {"col": column, "tile": place.along(0, target)})
+                      {"tile": tile_of(k_index, (c_index + s) % SIDE)})
+
+    def right(s, j, column):
+        source = tile_of((k_index + SIDE - j) % SIDE, (c_index + SIDE - s) % SIDE)
+        piece = chunk(q_ref, k_index) if s == 0 and j == 0 else slot(qall, source)
+        return remote(piece, slot(lall, source), r_send.at[s, j], r_recv.at[s, j], {"col": column})
+
+    def pass_right(s, j):
+        @pl.when(jnp.logical_not(last))
+        def _():
+            right(s, j, col + 1).start()
 
     def edge1(s):
         target = (place.x + s) % SIDE
-        return remote(chunk(edge_ref, target), slot(lall, place.tile), l2_send.at[SIDE - 2 + s], l1_recv.at[s],
+        return remote(chunk(edge_ref, target), slot(lall, place.tile), l1_send.at[s], l1_recv.at[s],
                       {"tile": place.along(0, target)})
 
     def l2(s):
@@ -229,15 +240,11 @@
         return pltpu.make_async_copy(chunk(edge_ref, place.x), slot(lall, place.tile), l1_recv.at[0])
 
     def send_chunk(index):
-        step = (index - place.y + SIDE) % SIDE
+        step = (index - k_index + SIDE) % SIDE
 
         @pl.when(step > 0)
         def _():
             q1(step).start()
-
-        @pl.when(jnp.logical_not(last))
-        def _():
-            l1(q_ref, (index - place.x + SIDE) % SIDE, col + 1).start()
 
     @pl.when(first)
     def _():
@@ -372,32 +379,30 @@
             lo = (k - i - 1) * NB
             s_ref[k * NB:k * NB + NB, k * NB:] = before - f32_dot(upper[:, lo:lo + NB].T, upper[:, lo:])
 
-    keep_q = pltpu.make_async_copy(chunk(q_ref, place.y), slot(qall, place.tile), keep_sem)
+    keep_q = pltpu.make_async_copy(chunk(q_ref, k_index), slot(qall, place.tile), keep_sem)
     keep_q.start()
     for s in steps:
         q2(s, 0).start()
+    pass_right(0, 0)
     for j in steps:
         q1(j).wait_recv()
         for s in steps:
             q2(s, j).start()
+        pass_right(0, j)
 
     @pl.when(first)
     def _():
         edge_own().wait()
         for s in steps:
             edge1(s).wait_recv()
-
-    @pl.when(jnp.logical_not(first))
-    def _():
-        for s in range(SIDE):
-            l1(q_ref, s, col).wait_recv()
-
-    for s in steps:
-        l2(s).start()
+        for s in steps:
+            l2(s).start()
+
     keep_q.wait()
-    for s in steps:
-        for j in range(SIDE):
+    for j in range(SIDE):
+        for s in steps:
             q2(s, j).wait_recv()
+            pass_right(s, j)
     part_k = wide // 2
     for r in range(legs):
         turned = qall[r].astype(jnp.float32).T.astype(jnp.bfloat16)
@@ -408,18 +413,20 @@
     for gather in sites:
         gather.finish()
 
-    def out(s):
-        target = (place.x + s) % SIDE
-        return remote(osend.at[pl.ds(pl.multiple_of(target * wide, wide), wide)],
-                      oall.at[:, pl.ds(pl.multiple_of(place.x * wide, wide), wide)],
-                      o_send.at[s - 1], o_recv.at[s - 1], {"tile": place.along(0, target)})
+    def out(i):
+        return remote(osend.at[i * wide:i * wide + wide],
+                      oall.at[:, pl.ds(pl.multiple_of(c_index * wide, wide), wide)],
+                      o_send.at[i], o_recv.at[c_index], {"tile": k_index * SIDE + i})
+
+    def out_wait(c):
+        return remote(osend.at[0:wide], oall.at[:, c * wide:c * wide + wide], o_send.at[0], o_recv.at[c], {"tile": OWNER})
 
     owner = place.tile == OWNER
     others = [t for t in range(tiles) if t != OWNER]
 
     def block(h):
-        return (pl.ds(pl.multiple_of(place.x * wide, wide), wide),
-                pl.ds(pl.multiple_of(place.y * wide + h * part_k, part_k), part_k))
+        return (pl.ds(pl.multiple_of(c_index * wide, wide), wide),
+                pl.ds(pl.multiple_of(k_index * wide + h * part_k, part_k), part_k))
 
     def gather(h, slot):
         return remote(tsend.at[h], across.at[block(h)], gather_send.at[h], gather_recv.at[h, slot], {"tile": OWNER})
@@ -462,19 +469,28 @@
                     low = (y - high.astype(jnp.float32)).astype(jnp.bfloat16)
                     rows = pl.ds(pl.multiple_of(g * 64, 64), 64)
                     for l in range(legs):
-                        yh[l, rows, :] = high[l * 64:l * 64 + 64]
-                        yl[l, rows, :] = low[l * 64:l * 64 + 64]
-
-            if h == 0:
-                @pl.when(piece == 0)
-                def _():
-                    for s in steps:
-                        l2(s).wait_recv()
-
+                        yh[piece, l, rows, :] = high[l * 64:l * 64 + 64]
+                        yl[piece, l, rows, :] = low[l * 64:l * 64 + 64]
+
+        if h == 0:
+            @pl.when(first)
+            def _():
+                for s in steps:
+                    l2(s).wait_recv()
+
+            @pl.when(jnp.logical_not(first))
+            def _():
+                for s in range(SIDE):
+                    for j in range(SIDE):
+                        right(s, j, col).wait_recv()
+
+        @pl.loop(0, width // wide)
+        def _(piece):
+            lanes = pl.ds(pl.multiple_of(piece * wide, wide), wide)
             for l in range(legs):
                 left = lall[l, lanes, :]
-                term = (jnp.dot(yh[l], left, preferred_element_type=jnp.float32)
-                        + jnp.dot(yl[l], left, preferred_element_type=jnp.float32))
+                term = (jnp.dot(yh[piece, l], left, preferred_element_type=jnp.float32)
+                        + jnp.dot(yl[piece, l], left, preferred_element_type=jnp.float32))
                 acc[...] = acc[...] + term
 
         osend[base:base + legs * part_k, :] = acc[...].astype(jnp.bfloat16)
@@ -493,10 +509,16 @@
         def _():
             gather(h, place.tile).start()
 
-    for s in steps:
-        out(s).start()
-    mine = pl.multiple_of(place.x * wide, wide)
-    oall[:, pl.ds(mine, wide)] = osend[pl.ds(mine, wide), :]
+    for i in range(SIDE):
+        there = k_index * SIDE + i
+
+        @pl.when(there != place.tile)
+        def _():
+            out(i).start()
+
+        @pl.when(there == place.tile)
+        def _():
+            oall[:, pl.ds(pl.multiple_of(c_index * wide, wide), wide)] = osend[i * wide:i * wide + wide, :]
 
     @pl.when(owner)
     def _():
@@ -532,8 +554,11 @@
         weighted = stage[...]
         env_ref[...] = weighted * scale_of(weighted)
 
-    for s in steps:
-        out(s).wait_recv()
+    for c in range(SIDE):
+        @pl.when(place.y * k_step + c * c_step != place.tile)
+        def _():
+            out_wait(c).wait_recv()
+
     out_ref[...] = oall[...]
 
     @pl.when(owner)
@@ -553,10 +578,13 @@
         for h in (0, 1):
             gather(h, place.tile).wait_send()
 
+    for i in range(SIDE):
+        @pl.when(k_index * SIDE + i != place.tile)
+        def _():
+            out(i).wait_send()
+
     for s in steps:
         q1(s).wait_send()
-        l2(s).wait_send()
-        out(s).wait_send()
         for j in range(SIDE):
             q2(s, j).wait_send()
 
@@ -564,11 +592,13 @@
     def _():
         for s in steps:
             edge1(s).wait_send()
+            l2(s).wait_send()
 
     @pl.when(jnp.logical_not(last))
     def _():
         for s in range(SIDE):
-            l1(q_ref, s, col + 1).wait_send()
+            for j in range(SIDE):
+                right(s, j, col + 1).wait_send()
 
 
 def absorb(site, sketch, amat, phys, edge, closing, left_edge, cols, tiles):
@@ -605,8 +635,8 @@
             vmem((legs, width, wide), bf16),
             vmem((legs * wide, width), bf16),
             vmem((legs * wide // 2, legs * wide), f32),
-            vmem((legs, legs * wide // 2, wide), bf16),
-            vmem((legs, legs * wide // 2, wide), bf16),
+            vmem((SIDE, legs, legs * wide // 2, wide), bf16),
+            vmem((SIDE, legs, legs * wide // 2, wide), bf16),
             vmem((legs * wide // 2, wide), f32),
             vmem((legs * wide, wide), bf16),
             vmem((legs * share, width), bf16),
@@ -628,8 +658,9 @@
             dma((SIDE - 1,)), dma((SIDE - 1,)),
             dma((SIDE - 1, SIDE)), dma((SIDE - 1, SIDE)),
             dma((SIDE,)), dma((SIDE,)),
-            dma((2 * SIDE - 2,)), dma((SIDE - 1,)),
             dma((SIDE - 1,)), dma((SIDE - 1,)),
+            dma((SIDE,)), dma((SIDE,)),
+            dma((SIDE, SIDE)), dma((SIDE, SIDE)),
         ],
         compiler_params=pltpu.CompilerParams(collective_id=0, has_side_effects=True, vmem_limit_bytes=62 << 20),
     )(site, sketch, amat, phys, edge, closing, left_edge.reshape(1, width))

time: 234 us -> 224 us (0.957)
  Pallas kernels: 226 us -> 216 us
    pallas_call x1, Pallas kernels: 226 us -> 216 us  [absorb(): pl.pallas_call(functools.partial(kernel, cols, tiles), out_shape=(jax.Sha...]
where the time goes in v3:
time: 224 us
  Pallas kernels  216 us (96%)
  local copies, waits for them, and re-layouts  7.2 us (3%)
    pallas_call x1, Pallas kernels, absorb(): pl.pallas_call(functools.partial(kernel, cols, tiles), out_shape=(jax.Sha...  216 us

profile of v3, /device:TPU:229, one launch (start us, length us, event | category | flops | bytes accessed | tf_op | source)
XLA Modules:
  0.0 223.6 jit_solution(11212496952047519624)
XLA Ops:
  0.6 0.0 copy-start.1
  0.6 0.0 copy-start
  0.6 2.1 copy.16
  2.7 0.0 copy-done.1
  2.7 0.7 reshape.22.amat_ref
  3.4 0.0 copy-done
  3.4 1.0 copy.15
  4.4 215.7 %shard_map.86 = (bf16[256,1024]{1,0:T(8,128)(2,1)}, f32[1,1024]{1,0:T(1,128)}) custom-call(bf16[4,64,1024]{2,1,0:T(8,128)(2,1)} %bitcast.20, bf16[64,1024]{1,0:T(8,128)(2,1)} %bitcast.24, f32[16,16]{1,0:T(8,128)} %reshape.22.amat_ref, bf16[4,4,1024]{2,1,0:T(4,128)(2,1)} %bitcast.25, bf16[4,64,1024]{2,1,0:T(8,128)(2,1)} %bitcast.21, f32[1,4]{1,0:T(1,128)} %close_ref.1, ...), custom_call_target="tpu_custom_call" | custom-call | tf_op jit(solution)/shard_map/pallas_call | solution.py:615
  220.1 2.2 %copy.12 = bf16[4,16,4,1024]{3,2,1,0:T(4,128)(2,1)} copy(bf16[4,16,4,1024]{3,1,2,0:T(8,128)(2,1)} %bitcast.23) | data formatting | bytes 1048576 | tf_op jit(solution)/shard_map/transpose | solution.py:676
  222.3 1.2 constant_dynamic-slice_fusion
  (2 shorter events, 0.0 us)
Async XLA Ops:
  0.6 2.1 copy-start.1
  0.6 2.8 %copy-start = (bf16[64,4,1024]{2,1,0:T(4,128)(2,1)S(1)}, bf16[64,4,1024]{2,1,0:T(4,128)(2,1)}, u32[]{:S(2)}) copy-start(bf16[64,4,1024]{2,1,0:T(4,128)(2,1)} %param.11) | copy-start | bytes 1572868
